TPU v7x, 256 devices: a whole 4x4x8 slice. The times are simulated.
256 devices in a mesh: seg: 32 (over x, z), tp: 8 (over y, core).
Axes of the slice: x: 4, y: 4, z: 8, core: 2. Of those that a mesh axis runs over, the one named last changes fastest.
Arguments:
- queries: bfloat16 [8192, 8192], P('seg', 'tp'), may hold values from -8 to 8
- keys_own: bfloat16 [8192, 1024], P('seg', 'tp'), may hold values from -8 to 8
- values_own: bfloat16 [8192, 1024], P('seg', 'tp'), may hold values from -6 to 6
- out_grad: bfloat16 [8192, 8192], P('seg', 'tp'), may hold values from -6 to 6
- summary_states: bfloat16 [1600, 8192], P('seg'), may hold values from -6 to 6
- w_key: bfloat16 [8192, 1024], P(None, 'tp'), may hold values from -0.0625 to 0.0625
- w_value: bfloat16 [8192, 1024], P(None, 'tp'), may hold values from -0.0625 to 0.0625
- summary_grad: bfloat16 [1600, 8192], P('seg', 'tp'), may hold values from -6 to 6
Outputs:
- query_grad: bfloat16 [8192, 8192], P('seg', 'tp')
- key_grad: bfloat16 [8192, 1024], P('seg', 'tp')
- value_grad: bfloat16 [8192, 1024], P('seg', 'tp')
- state_grad: bfloat16 [1600, 8192], P('seg', 'tp')
All inputs are finite; a program needn't handle non-finite values.
Results may differ from a plain program's by a relative error of at most 0.023.
Values may be sent and summed in bfloat16 or wider, within the bound.
A program may use at most 256 MiB of HBM per device.

v0:
```python
import jax
import jax.numpy as jnp
from jax import lax
from jax.sharding import PartitionSpec as P

HEADS = 64
KVH = 8
HD = 128


def per_device(
    queries, keys_own, values_own, out_grad, summary_states, w_key, w_value, summary_grad
):
    rows = queries.shape[0]
    kv_local = keys_own.shape[1] // HD
    group = HEADS // KVH
    scale = HD ** (-0.5)
    count = summary_states.shape[0]
    segments = lax.axis_size("seg")
    position = lax.axis_index("seg")
    nsum = count * segments
    nkeys = nsum + rows
    width = kv_local * HD
    projected = jnp.concatenate(
        [
            jnp.dot(summary_states, w_key, preferred_element_type=jnp.float32).astype(jnp.bfloat16),
            jnp.dot(summary_states, w_value, preferred_element_type=jnp.float32).astype(
                jnp.bfloat16
            ),
        ],
        axis=1,
    )
    everyone = lax.all_gather(projected, "seg", axis=0, tiled=True)
    keys_all = jnp.concatenate([everyone[:, :width], keys_own], 0)
    vals_all = jnp.concatenate([everyone[:, width:], values_own], 0)
    row_pos = jnp.arange(rows)[:, None]
    col_pos = jnp.arange(nkeys)[None, :]
    visible = jnp.where(col_pos < nsum, col_pos < position * count, col_pos - nsum <= row_pos)
    query_heads = queries.reshape(rows, kv_local * group, HD).transpose(1, 0, 2)
    grad_heads = out_grad.reshape(rows, kv_local * group, HD).transpose(1, 0, 2)
    contract_last = (((1,), (1,)), ((), ()))
    contract_first = (((0,), (0,)), ((), ()))

    def head_step(carry, inputs):
        key_acc, val_acc = carry
        query_head, grad_head = inputs
        scores = (
            lax.dot_general(query_head, keys_all, contract_last, preferred_element_type=jnp.float32)
            * scale
        )
        scores = jnp.where(visible, scores, -jnp.inf)
        probs = jnp.exp(scores - jnp.max(scores, axis=-1, keepdims=True))
        probs = probs / jnp.sum(probs, axis=-1, keepdims=True)
        probs_b = probs.astype(jnp.bfloat16)
        attn = jnp.dot(probs_b, vals_all, preferred_element_type=jnp.float32)
        delta = jnp.sum(grad_head.astype(jnp.float32) * attn, axis=-1)
        dprobs = lax.dot_general(
            grad_head, vals_all, contract_last, preferred_element_type=jnp.float32
        )
        dscores = (probs * (dprobs - delta[:, None])).astype(jnp.bfloat16)
        dquery = (jnp.dot(dscores, keys_all, preferred_element_type=jnp.float32) * scale).astype(
            jnp.bfloat16
        )
        key_acc = key_acc + lax.dot_general(
            dscores, query_head, contract_first, preferred_element_type=jnp.float32
        )
        val_acc = val_acc + lax.dot_general(
            probs_b, grad_head, contract_first, preferred_element_type=jnp.float32
        )
        return ((key_acc, val_acc), dquery)

    zeros = jnp.zeros((nkeys, HD), jnp.float32)
    (key_acc, val_acc), dquery = lax.scan(head_step, (zeros, zeros), (query_heads, grad_heads))
    key_sums = [key_acc * scale]
    value_sums = [val_acc]
    query_grad = dquery.transpose(1, 0, 2).reshape(rows, kv_local * group * HD)
    key_grad = jnp.concatenate([acc[nsum:] for acc in key_sums], 1).astype(jnp.bfloat16)
    value_grad = jnp.concatenate([acc[nsum:] for acc in value_sums], 1).astype(jnp.bfloat16)
    summary_terms = jnp.concatenate(
        [acc[:nsum] for acc in key_sums] + [acc[:nsum] for acc in value_sums], 1
    )
    emitted = lax.psum_scatter(
        summary_terms.astype(jnp.bfloat16), "seg", scatter_dimension=0, tiled=True
    )
    partial_state = lax.dot_general(
        emitted[:, :width], w_key, contract_last, preferred_element_type=jnp.float32
    )
    partial_state = partial_state + lax.dot_general(
        emitted[:, width:], w_value, contract_last, preferred_element_type=jnp.float32
    )
    shared = lax.psum_scatter(
        partial_state.astype(jnp.bfloat16), "tp", scatter_dimension=1, tiled=True
    ).astype(jnp.float32)
    state_grad = (shared + summary_grad.astype(jnp.float32)).astype(jnp.bfloat16)
    return (query_grad, key_grad, value_grad, state_grad)


def solution(mesh):
    placed = (
        P("seg", "tp"),
        P("seg", "tp"),
        P("seg", "tp"),
        P("seg", "tp"),
        P("seg", None),
        P(None, "tp"),
        P(None, "tp"),
        P("seg", "tp"),
    )
    return jax.shard_map(
        per_device,
        mesh=mesh,
        in_specs=placed,
        out_specs=(P("seg", "tp"), P("seg", "tp"), P("seg", "tp"), P("seg", "tp")),
        check_vma=False,
    )
```

profile of v0, /device:TPU:6, one launch (start us, length us, event | category | flops | bytes accessed | tf_op | source)
XLA Modules:
  0.0 369.8 jit_solution(2039793102110522160)
XLA Ops:
  7.3 2.5 convolution_convert_fusion
  10.4 52.5 %all-gather = bf16[32,50,256]{2,1,0:T(8,128)(2,1)S(1)} all-gather(bf16[1,50,256]{2,1,0:T(8,128)(2,1)S(1)} %maximum_bitcast_fusion), channel_id=1, replica_groups=mesh['seg'=32,'tp'=8] {'seg'}, dimensions={0}, use_global_device_ids=true | all-gather | bytes 844800 | tf_op jit(solution)/shard_map/all_gather | solution.py:33
  70.2 105.0 %while.15 = (s32[]{:T(128)}, f32[1856,128]{1,0:T(8,128)}, f32[1856,128]{1,0:T(8,128)}, bf16[8,256,128]{2,1,0:T(8,128)(2,1)}, bf16[8,256,128]{1,2,0:T(8,128)(2,1)...) while((s32[]{:T(128)}, f32[1856,128]{1,0:T(8,128)}, ...), condition=%wide.region_4.5_spmd.clone, body=%wide.region_0.4_spmd.clone.sunk | while | flops 738049280 | bytes 25123396 | solution.py:73
  76.8 2.6 convolution_add_fusion.5
  89.3 2.9 convolution_add_fusion.5
  93.4 2.6 convolution_add_fusion.6
  102.5 2.9 convolution_add_fusion.5
  106.6 2.6 convolution_add_fusion.6
  113.4 2.3 fusion.79
  115.7 2.9 convolution_add_fusion.5
  119.8 2.6 convolution_add_fusion.6
  126.6 2.3 fusion.79
  129.0 2.9 convolution_add_fusion.5
  133.0 2.6 convolution_add_fusion.6
  139.8 2.3 fusion.79
  142.2 2.9 convolution_add_fusion.5
  146.2 2.6 convolution_add_fusion.6
  155.4 2.9 convolution_add_fusion.5
  159.4 2.6 convolution_add_fusion.6
  168.6 2.9 convolution_add_fusion.5
  172.6 2.6 convolution_add_fusion.6
  180.2 143.3 %all-reduce.3.cloned.1.call-done = bf16[1600,256]{1,0:T(8,128)(2,1)} async-done(((bf16[1600,256]{1,0:T(8,128)(2,1)}), bf16[1600,256]{1,0:T(8,128)(2,1)}) %all-reduce.3.cloned.1.call-update) | async-done | bytes 819216
  325.6 3.0 fusion.25
  331.9 29.5 %reduce-scatter.2.cloned.1.call-done = bf16[50,1024]{1,0:T(8,128)(2,1)} async-done(((bf16[50,8192]{1,0:T(8,128)(2,1)}), bf16[50,1024]{1,0:T(8,128)(2,1)}) %reduce-scatter.2.cloned.1.call-update) | async-done | bytes 102416 | tf_op jit(solution)/shard_map/reduce_scatter | solution.py:91
  (119 shorter events, 75.5 us)
Async XLA Ops:
  7.2 2.6 copy-start
  7.2 2.7 copy-start.3
  7.2 316.2 %all-reduce.3.cloned.1.call-start = ((), (), s32[]{:S(2)}) async-start(), calls=%async_computation.2 | async-start | bytes 1638400
  64.0 5.3 %copy-start.6 = (bf16[256,128]{1,0:T(8,128)(2,1)S(1)}, bf16[256,128]{1,0:T(8,128)(2,1)}, u32[]{:S(2)}) copy-start(bf16[256,128]{1,0:T(8,128)(2,1)} %param.11) | copy-start | bytes 196612
  64.0 5.3 %copy-start.7 = (bf16[256,128]{1,0:T(8,128)(2,1)S(1)}, bf16[256,128]{1,0:T(8,128)(2,1)}, u32[]{:S(2)}) copy-start(bf16[256,128]{1,0:T(8,128)(2,1)} %param.12) | copy-start | bytes 196612
  72.2 1.0 copy-start.4
  76.8 2.6 copy-start.1
  84.8 1.0 copy-start.4
  89.3 3.0 copy-start.1
  98.0 1.0 copy-start.4
  102.5 2.9 copy-start.1
  111.2 1.0 copy-start.4
  115.7 2.9 copy-start.1
  124.4 1.0 copy-start.4
  128.9 3.0 copy-start.1
  137.6 1.0 copy-start.4
  142.2 2.9 copy-start.1
  155.4 2.9 copy-start.1
  164.0 1.0 copy-start.4
  168.6 2.9 copy-start.1
  177.8 1.1 copy-start.8
  178.8 182.5 %reduce-scatter.2.cloned.1.call-start = ((), (), s32[]{:S(2)}) async-start(), calls=%async_computation.1 | async-start | bytes 1032192 | tf_op jit(solution)/shard_map/reduce_scatter | solution.py:91
  323.4 2.2 copy-start.2
  328.7 32.7 %copy-start.5 = (bf16[50,1024]{1,0:T(8,128)(2,1)S(1)}, bf16[50,1024]{1,0:T(8,128)(2,1)}, u32[]{:S(2)}) copy-start(bf16[50,1024]{1,0:T(8,128)(2,1)} %param.17) | copy-start | bytes 307204
  (1 other events, 1.0 us)
Sparse Core Ops, SparseCore 0:
  179.0 144.4 all-reduce.2
  328.8 32.4 reduce-scatter.1
where the time goes:
time: 372 us; the launch traced here: 370 us
  waiting for transfers between devices  173 us (47%)
  matrix products  102 us (27%)
  blocking collectives  52.5 us (14%)
  local copies, waits for them, and re-layouts  16.2 us (4%)
  between operations  14.8 us (4%)
  other arithmetic  11 us (3%)
    unnamed x3, waiting for transfers between devices  143 us
    all_gather x1, blocking collectives, per_device(): everyone = lax.all_gather(projected, 'seg', axis=0, tiled=True)  52.5 us
    reduce_scatter x1, waiting for transfers between devices, per_device(): lax.psum_scatter(partial_state.astype(jnp.bfloat16), 'tp', scatter_dimens...  29.5 us
    dot_general x8, matrix products, head_step(): lax.dot_general(dscores, query_head, contract_first, preferred_element_ty...  23.3 us
    dot_general x8, matrix products, head_step(): lax.dot_general(probs_b, grad_head, contract_first, preferred_element_typ...  20.5 us
    dot_general x8, matrix products, head_step(): lax.dot_general(grad_head, vals_all, contract_last, preferred_element_typ...  18.6 us
    dot_general x8, matrix products, head_step(): lax.dot_general(query_head, keys_all, contract_last, preferred_element_ty...  13.3 us
    dot_general x8, matrix products, head_step(): attn = jnp.dot(probs_b, vals_all, preferred_element_type=jnp.float32)  9.62 us
  transfers between devices with their start and end apart: 2, of which 2 were waited for; matrix products, arithmetic and copies ran while one was open for 1% of the time, Pallas kernels for 0%

commit v1 on v0

--- a/solution.py
+++ b/solution.py
@@ -30,7 +30,10 @@
         ],
         axis=1,
     )
-    everyone = lax.all_gather(projected, "seg", axis=0, tiled=True)
+    everyone = jnp.concatenate(
+        lax.all_to_all(jnp.stack([projected for _ in range(lax.axis_size("seg"))], 0), "seg", 0, 0),
+        0,
+    )
     keys_all = jnp.concatenate([everyone[:, :width], keys_own], 0)
     vals_all = jnp.concatenate([everyone[:, width:], values_own], 0)
     row_pos = jnp.arange(rows)[:, None]

time: 372 us -> 352 us (0.946)
  blocking collectives: 52.5 us -> 0 us
  waiting for transfers between devices: 173 us -> 194 us
  starting transfers between devices: 0.08 us -> 11.7 us
    all_gather x1 -> x0, blocking collectives: 52.5 us -> none  [per_device(): everyone = lax.all_gather(projected, 'seg', axis=0, tiled=True)]
    all_to_all x0 -> x1, waiting for transfers between devices: none -> 20.6 us  [per_device(): lax.all_to_all(jnp.stack([projected for _ in range(lax.axis_size('seg'))]...]
    all_to_all x0 -> x1, starting transfers between devices: none -> 11.6 us  [per_device(): lax.all_to_all(jnp.stack([projected for _ in range(lax.axis_size('seg'))]...]
  transfers between devices with their start and end apart: 2 -> 3, of which waited for: 2 -> 3; matrix products, arithmetic and copies ran while one was open for 1% -> 2% of each run, Pallas kernels for 0% -> 0%
where the time goes in v1:
time: 352 us; the launch traced here: 349 us
  waiting for transfers between devices  194 us (55%)
  matrix products  102 us (29%)
  local copies, waits for them, and re-layouts  16.2 us (5%)
  between operations  14.9 us (4%)
  starting transfers between devices  11.7 us (3%)
  other arithmetic  11 us (3%)
    unnamed x3, waiting for transfers between devices  143 us
    reduce_scatter x1, waiting for transfers between devices, per_device(): lax.psum_scatter(partial_state.astype(jnp.bfloat16), 'tp', scatter_dimens...  29.4 us
    dot_general x8, matrix products, head_step(): lax.dot_general(dscores, query_head, contract_first, preferred_element_ty...  23.1 us
    all_to_all x1, waiting for transfers between devices, per_device(): lax.all_to_all(jnp.stack([projected for _ in range(lax.axis_size('seg'))]...  20.6 us
    dot_general x8, matrix products, head_step(): lax.dot_general(probs_b, grad_head, contract_first, preferred_element_typ...  20.5 us
    dot_general x8, matrix products, head_step(): lax.dot_general(grad_head, vals_all, contract_last, preferred_element_typ...  18.4 us
    dot_general x8, matrix products, head_step(): lax.dot_general(query_head, keys_all, contract_last, preferred_element_ty...  13.3 us
    all_to_all x1, starting transfers between devices, per_device(): lax.all_to_all(jnp.stack([projected for _ in range(lax.axis_size('seg'))]...  11.6 us
  transfers between devices with their start and end apart: 3, of which 3 were waited for; matrix products, arithmetic and copies ran while one was open for 2% of the time, Pallas kernels for 0%

profile of v1, /device:TPU:6, one launch (start us, length us, event | category | flops | bytes accessed | tf_op | source)
XLA Modules:
  0.0 349.4 jit_solution(14604607582383560026)
XLA Ops:
  7.2 2.5 convolution_convert_fusion
  11.4 11.6 %all-to-all-start = ((bf16[32,50,256]{2,1,0:T(8,128)(2,1)}), bf16[32,50,256]{2,1,0:T(8,128)(2,1)S(1)}, u32[]{:S(2)}, u32[]{:S(2)}) async-start(bf16[32,50,256]{2,1,0:T(8,128)(2,1)} %stack.2), calls=%async_computation | async-start | bytes 1835008 | tf_op jit(solution)/shard_map/all_to_all | solution.py:34
  26.2 20.6 %all-to-all-done = bf16[32,50,256]{2,1,0:T(8,128)(2,1)S(1)} async-done(((bf16[32,50,256]{2,1,0:T(8,128)(2,1)}), bf16[32,50,256]{2,1,0:T(8,128)(2,1)S(1)}, u32[]{:S(2)}, u32[]{:S(2)}) %all-to-all-start) | async-done | bytes 819232 | tf_op jit(solution)/shard_map/all_to_all | solution.py:34
  50.0 104.8 %while.15 = (s32[]{:T(128)}, f32[1856,128]{1,0:T(8,128)}, f32[1856,128]{1,0:T(8,128)}, bf16[8,256,128]{2,1,0:T(8,128)(2,1)}, bf16[8,256,128]{1,2,0:T(8,128)(2,1)...) while((s32[]{:T(128)}, f32[1856,128]{1,0:T(8,128)}, ...), condition=%wide.region_4.5_spmd.clone, body=%wide.region_0.4_spmd.clone.sunk | while | flops 738049280 | bytes 25123396 | solution.py:76
  56.5 2.6 convolution_add_fusion.5
  66.7 2.3 fusion.79
  69.1 2.9 convolution_add_fusion.5
  73.1 2.6 convolution_add_fusion.6
  82.2 2.9 convolution_add_fusion.5
  86.3 2.6 convolution_add_fusion.6
  95.4 2.9 convolution_add_fusion.5
  99.4 2.6 convolution_add_fusion.6
  108.6 2.9 convolution_add_fusion.5
  112.6 2.6 convolution_add_fusion.6
  121.8 2.9 convolution_add_fusion.5
  125.8 2.6 convolution_add_fusion.6
  135.0 2.9 convolution_add_fusion.5
  139.0 2.6 convolution_add_fusion.6
  145.9 2.3 fusion.79
  148.2 2.9 convolution_add_fusion.5
  152.2 2.6 convolution_add_fusion.6
  159.7 143.4 %all-reduce.3.cloned.1.call-done = bf16[1600,256]{1,0:T(8,128)(2,1)} async-done(((bf16[1600,256]{1,0:T(8,128)(2,1)}), bf16[1600,256]{1,0:T(8,128)(2,1)}) %all-reduce.3.cloned.1.call-update) | async-done | bytes 819216
  305.3 3.0 fusion.25
  311.6 29.4 %reduce-scatter.2.cloned.1.call-done = bf16[50,1024]{1,0:T(8,128)(2,1)} async-done(((bf16[50,8192]{1,0:T(8,128)(2,1)}), bf16[50,1024]{1,0:T(8,128)(2,1)}) %reduce-scatter.2.cloned.1.call-update) | async-done | bytes 102416 | tf_op jit(solution)/shard_map/reduce_scatter | solution.py:94
  (123 shorter events, 77.7 us)
Async XLA Ops:
  7.2 2.5 copy-start
  7.2 2.7 copy-start.3
  10.4 12.7 %copy-start.4 = (bf16[256,1024]{1,0:T(8,128)(2,1)S(1)}, bf16[256,1024]{1,0:T(8,128)(2,1)}, u32[]{:S(2)}) copy-start(bf16[256,1024]{1,0:T(8,128)(2,1)} %param.10) | copy-start | bytes 1572868
  11.4 35.4 %all-to-all-start = ((bf16[32,50,256]{2,1,0:T(8,128)(2,1)}), bf16[32,50,256]{2,1,0:T(8,128)(2,1)S(1)}, u32[]{:S(2)}, u32[]{:S(2)}) async-start(bf16[32,50,256]{2,1,0:T(8,128)(2,1)} %stack.2), calls=%async_computation | async-start | bytes 1835008 | tf_op jit(solution)/shard_map/all_to_all | solution.py:34
  23.0 280.1 %all-reduce.3.cloned.1.call-start = ((), (), s32[]{:S(2)}) async-start(), calls=%async_computation.3 | async-start | bytes 1638400
  26.2 23.0 %copy-start.7 = (bf16[256,128]{1,0:T(8,128)(2,1)S(1)}, bf16[256,128]{1,0:T(8,128)(2,1)}, u32[]{:S(2)}) copy-start(bf16[256,128]{1,0:T(8,128)(2,1)} %param.11) | copy-start | bytes 196612
  26.2 23.0 %copy-start.8 = (bf16[256,128]{1,0:T(8,128)(2,1)S(1)}, bf16[256,128]{1,0:T(8,128)(2,1)}, u32[]{:S(2)}) copy-start(bf16[256,128]{1,0:T(8,128)(2,1)} %param.12) | copy-start | bytes 196612
  52.0 1.0 copy-start.5
  56.5 2.6 copy-start.1
  69.1 2.9 copy-start.1
  77.7 1.0 copy-start.5
  82.2 2.9 copy-start.1
  95.4 2.9 copy-start.1
  104.0 1.0 copy-start.5
  108.6 2.9 copy-start.1
  117.2 1.0 copy-start.5
  121.8 2.9 copy-start.1
  130.4 1.0 copy-start.5
  135.0 2.9 copy-start.1
  148.2 2.9 copy-start.1
  157.4 1.1 copy-start.9
  158.4 182.6 %reduce-scatter.2.cloned.1.call-start = ((), (), s32[]{:S(2)}) async-start(), calls=%async_computation.2 | async-start | bytes 1032192 | tf_op jit(solution)/shard_map/reduce_scatter | solution.py:94
  303.1 2.2 copy-start.2
  308.4 32.6 %copy-start.6 = (bf16[50,1024]{1,0:T(8,128)(2,1)S(1)}, bf16[50,1024]{1,0:T(8,128)(2,1)}, u32[]{:S(2)}) copy-start(bf16[50,1024]{1,0:T(8,128)(2,1)} %param.17) | copy-start | bytes 307204
  (3 other events, 3.1 us)
Sparse Core Ops, SparseCore 0:
  158.5 144.5 all-reduce.2
  308.5 32.4 reduce-scatter.1
